TPU v7x, 32 devices: a whole 2x2x4 slice. The times are simulated.
32 devices in a mesh: dp: 16 (over z, y, core), space: 2 (over x).
Axes of the slice: x: 2, y: 2, z: 4, core: 2. Of those that a mesh axis runs over, the one named last changes fastest.
Arguments:
- volumes: bfloat16 [16, 32, 8, 8, 128], P('dp', None, 'space'), may hold values from -6 to 6
- w_first: bfloat16 [864, 64], P('dp'), may hold values from -0.21875 to 0.21875
- w_second: bfloat16 [1728, 128], P('dp'), may hold values from -0.4375 to 0.4375
- cotangent: bfloat16 [16, 128, 2, 2, 32], P('dp', None, 'space'), may hold values from -96 to 96
Outputs:
- pooled: bfloat16 [16, 128, 2, 2, 32], P('dp', None, 'space')
- volume_grad: bfloat16 [16, 32, 8, 8, 128], P('dp', None, 'space')
- grad_first: float32 [864, 64], P('dp')
- grad_second: float32 [1728, 128], P('dp')
All inputs are finite; a program needn't handle non-finite values.
Results may differ from a plain program's by a relative error of at most 0.023.
Values may be sent and summed in bfloat16 or wider, within the bound.
No kernel may reach another device: no remote copies, remote signals or barrier semaphores. Data moves between devices by JAX's collectives and lax.ppermute only.
A program may use at most 128 MiB of HBM per device.

v0:
```python
import jax
import jax.numpy as jnp
from jax import lax
from jax.sharding import PartitionSpec as P


def with_halo(block, sides, width):
    for axis, dim in sides:
        count = lax.axis_size(axis)
        forward = [(i, i + 1) for i in range(count - 1)]
        backward = [(target, source) for source, target in forward]
        low = lax.ppermute(
            lax.slice_in_dim(block, block.shape[dim] - width, None, axis=dim), axis, forward
        )
        high = lax.ppermute(lax.slice_in_dim(block, 0, width, axis=dim), axis, backward)
        block = jnp.concatenate([low, block, high], axis=dim)
    return block


def pad_sides(field):
    return jnp.pad(field, ((0, 0), (0, 0), (0, 0), (1, 1), (1, 1)))


def conv_forward(padded, weight):
    samples_here, in_width, depth_padded, extent_y, extent_z = padded.shape
    extent_x = depth_padded - 2
    out_width = weight.shape[1]
    framed = pad_sides(padded)
    kernel = weight.reshape(3, 3, 3, in_width, out_width)
    summed = jnp.zeros((samples_here, out_width, extent_x, extent_y, extent_z), jnp.float32)
    for along_x in range(3):
        for along_y in range(3):
            for along_z in range(3):
                window = framed[
                    :,
                    :,
                    along_x : along_x + extent_x,
                    along_y : along_y + extent_y,
                    along_z : along_z + extent_z,
                ]
                summed = summed + jnp.einsum(
                    "sixyz,io->soxyz",
                    window,
                    kernel[along_x, along_y, along_z],
                    preferred_element_type=jnp.float32,
                )
    return summed


def conv_input_grad(padded, weight, in_width):
    samples_here, out_width, depth_padded, extent_y, extent_z = padded.shape
    extent_x = depth_padded - 2
    framed = pad_sides(padded)
    kernel = weight.reshape(3, 3, 3, in_width, out_width)
    summed = jnp.zeros((samples_here, in_width, extent_x, extent_y, extent_z), jnp.float32)
    for along_x in range(3):
        for along_y in range(3):
            for along_z in range(3):
                window = framed[
                    :,
                    :,
                    2 - along_x : 2 - along_x + extent_x,
                    2 - along_y : 2 - along_y + extent_y,
                    2 - along_z : 2 - along_z + extent_z,
                ]
                summed = summed + jnp.einsum(
                    "soxyz,io->sixyz",
                    window,
                    kernel[along_x, along_y, along_z],
                    preferred_element_type=jnp.float32,
                )
    return summed


def conv_weight_grad(padded, grads):
    samples_here, in_width, depth_padded, extent_y, extent_z = padded.shape
    extent_x = depth_padded - 2
    framed = pad_sides(padded)
    pieces = []
    for along_x in range(3):
        for along_y in range(3):
            for along_z in range(3):
                window = framed[
                    :,
                    :,
                    along_x : along_x + extent_x,
                    along_y : along_y + extent_y,
                    along_z : along_z + extent_z,
                ]
                pieces.append(
                    jnp.einsum("sixyz,soxyz->io", window, grads, preferred_element_type=jnp.float32)
                )
    return jnp.stack(pieces).reshape(27 * in_width, grads.shape[1])


def pooling(field):
    samples_here, width, extent_x, extent_y, extent_z = field.shape
    blocks = field.reshape(
        samples_here, width, extent_x // 2, 2, extent_y // 2, 2, extent_z // 2, 2
    )
    return jnp.mean(blocks, axis=(3, 5, 7))


def spread_up(field):
    samples_here, width, extent_x, extent_y, extent_z = field.shape
    blocks = jnp.broadcast_to(
        field[:, :, :, None, :, None, :, None],
        (samples_here, width, extent_x, 2, extent_y, 2, extent_z, 2),
    )
    return blocks.reshape(samples_here, width, 2 * extent_x, 2 * extent_y, 2 * extent_z)


def silu_slope(values):
    sigma = jax.nn.sigmoid(values)
    return sigma * (1.0 + values * (1.0 - sigma))


def local(volumes, w_first, w_second, cotangent):
    kernel_one, kernel_two = (
        lax.all_gather(w_first, "dp", axis=0, tiled=True),
        lax.all_gather(w_second, "dp", axis=0, tiled=True),
    )
    in_width = volumes.shape[1]
    mid_width = kernel_one.shape[1]
    count_one = lax.axis_size("dp") * lax.axis_size("space") * (volumes.size // in_width)
    factor_one = float(count_one) ** (-0.5)
    factor_two = float(count_one // 8) ** (-0.5)
    input_padded = with_halo(volumes, (("space", 2),), 1)
    first_pre = conv_forward(input_padded, kernel_one)
    first_pool = pooling(jax.nn.silu(first_pre)).astype(jnp.bfloat16)
    pool_padded = with_halo(first_pool, (("space", 2),), 1)
    second_pre = conv_forward(pool_padded, kernel_two)
    pooled = pooling(jax.nn.silu(second_pre)).astype(jnp.bfloat16)
    second_delta = (
        spread_up(cotangent.astype(jnp.float32)) * 0.125 * silu_slope(second_pre)
    ).astype(jnp.bfloat16)
    grad_two = conv_weight_grad(pool_padded, second_delta) * factor_two
    delta_padded = with_halo(second_delta, (("space", 2),), 1)
    pool_grad = conv_input_grad(delta_padded, kernel_two, mid_width).astype(jnp.bfloat16)
    first_delta = (spread_up(pool_grad.astype(jnp.float32)) * 0.125 * silu_slope(first_pre)).astype(
        jnp.bfloat16
    )
    grad_one = conv_weight_grad(input_padded, first_delta) * factor_one
    first_padded = with_halo(first_delta, (("space", 2),), 1)
    volume_grad = conv_input_grad(first_padded, kernel_one, in_width).astype(jnp.bfloat16)
    rows_one, rows_two = (
        lax.psum_scatter(
            grad_one.astype(jnp.bfloat16), "dp", scatter_dimension=0, tiled=True
        ).astype(jnp.float32),
        lax.psum_scatter(
            grad_two.astype(jnp.bfloat16), "dp", scatter_dimension=0, tiled=True
        ).astype(jnp.float32),
    )
    share_one, share_two = (
        lax.psum(rows_one.astype(jnp.bfloat16), "space").astype(jnp.float32),
        lax.psum(rows_two.astype(jnp.bfloat16), "space").astype(jnp.float32),
    )
    return (pooled, volume_grad, share_one, share_two)


def solution(mesh):
    return jax.shard_map(
        local,
        mesh=mesh,
        in_specs=(
            P("dp", None, "space", None, None),
            P("dp", None),
            P("dp", None),
            P("dp", None, "space", None, None),
        ),
        out_specs=(
            P("dp", None, "space", None, None),
            P("dp", None, "space", None, None),
            P("dp", None),
            P("dp", None),
        ),
        check_vma=False,
    )
```

profile of v0, /device:TPU:18, one launch (start us, length us, event | category | flops | bytes accessed | tf_op | source)
XLA Modules:
  0.0 181.7 jit_solution(16908317429202196970)
XLA Ops:
  0.6 1.1 copy.81
  1.7 1.3 collective-permute-start
  3.0 4.5 %collective-permute-start.1 = (bf16[1,32,1,8,128]{4,1,3,2,0:T(8,128)(2,1)S(1)}, bf16[1,32,1,8,128]{4,1,3,2,0:T(8,128)(2,1)S(1)}, u32[]{:S(2)}, u32[]{:S(2)}) collective-permute-start(bf16[1,32,1,8,128]{4,1,3,2,0:T(8,128)(2,1)S(1)} %get-tuple-element.27), channel_id=1, source_target_pairs={{1,0},{3,2},{5,4},{7,6},{9,8},{11,10},{13,12},{15,14},{17,16},{19,... | collective-permute-start | bytes 196616 | tf_op jit(solution)/shard_map/ppermute | solution.py:15
  7.6 0.7 multiply_bitcast_fusion
  8.3 16.8 %all-gather = bf16[16,54,64]{2,1,0:T(8,128)(2,1)S(1)} all-gather(bf16[1,54,64]{2,1,0:T(8,128)(2,1)} %bitcast.1526), channel_id=1, replica_groups=mesh['dp'=16,'space'=2] {'dp'}, dimensions={0}, use_global_device_ids=true | all-gather | bytes 117504 | tf_op jit(solution)/shard_map/all_gather | solution.py:120
  25.2 0.4 select_maximum_fusion.2
  26.0 0.4 fusion.173
  26.4 0.4 convolution_bitcast_fusion.10
  27.1 0.4 convolution_bitcast_fusion.6
  27.5 0.4 convolution_bitcast_fusion.7
  28.2 0.4 convolution_bitcast_fusion.9
  29.0 0.4 convolution_bitcast_fusion.1
  30.5 0.4 convolution_add_fusion.10
  31.9 0.4 convolution_add_fusion.6
  33.0 0.4 convolution_add_fusion.3
  33.4 0.4 convolution_add_fusion.2
  34.7 0.6 fusion.17
  35.7 1.9 %fusion.134 = (f32[64,4,8,128]{3,0,2,1:T(8,128)}, f32[64,4,8,128]{3,0,2,1:T(8,128)}) fusion(f32[64,4,8,128]{3,0,2,1:T(8,128)S(1)} %convolution_bitcast_fusion, f32[64,4,8,128]{3,0,2,1:T(8,128)S(1)} %convolution_bitcast_fusion.1, f32[64,4,8,128]{3,0,2,1:T(8,128)S(1)} %convolution_bitcast_fusion.2, f32[64,4,8,128]{3,0,2,1:T(8,128)S(1)} %convolution_bitcast_fusion.3, ...), kind=kOutput, calls=%fused_computation.293 | convolution fusion | flops 19267584 | bytes 7675904 | tf_op jit(solution)/shard_map/sixyz,io->soxyz/dot_general | solution.py:41
  37.6 1.8 %copy.87 = f32[64,4,8,128]{0,3,2,1:T(8,128)S(1)} copy(f32[64,4,8,128]{3,0,2,1:T(8,128)} %get-tuple-element.32) | data formatting | bytes 2097152 | tf_op jit(solution)/shard_map/jit(silu)/mul | solution.py:130
  39.5 2.4 %reduce_sum.21 = f32[64,2,4,64]{0,3,2,1:T(8,128)} reduce(f32[64,2,2,4,2,64,2]{0,6,5,4,3,2,1:T(2,128)S(1)} %bitcast.1517, f32[]{:T(128)} %constant.8.clone.1), dimensions={2,4,6}, to_apply=%region_0.1 | reduce | flops 229376 | bytes 1179652 | tf_op jit(solution)/shard_map/reduce_sum | solution.py:101
  41.9 1.0 fusion.210
  42.9 1.3 collective-permute-start.2
  44.2 4.5 %collective-permute-start.3 = (bf16[1,64,1,4,64]{1,4,3,2,0:T(8,128)(2,1)S(1)}, bf16[1,64,1,4,64]{1,4,3,2,0:T(8,128)(2,1)S(1)}, u32[]{:S(2)}, u32[]{:S(2)}) collective-permute-start(bf16[1,64,1,4,64]{1,4,3,2,0:T(8,128)(2,1)S(1)} %get-tuple-element.31), channel_id=1, source_target_pairs={{1,0},{3,2},{5,4},{7,6},{9,8},{11,10},{13,12},{15,14},{17,16},{19,... | collective-permute-start | bytes 98312 | tf_op jit(solution)/shard_map/ppermute | solution.py:15
  48.7 18.7 %all-gather.1 = bf16[16,108,128]{2,1,0:T(8,128)(2,1)S(1)} all-gather(bf16[1,108,128]{2,1,0:T(8,128)(2,1)S(1)} %bitcast.1525), channel_id=1, replica_groups=mesh['dp'=16,'space'=2] {'dp'}, dimensions={0}, use_global_device_ids=true | all-gather | bytes 470016 | tf_op jit(solution)/shard_map/all_gather | solution.py:121
  67.5 0.6 dynamic-slice.6
  80.2 0.9 multiply_convert_fusion.1
  81.1 1.3 collective-permute-start.4
  82.4 4.5 %collective-permute-start.5 = (bf16[1,128,1,4,64]{1,4,3,2,0:T(8,128)(2,1)S(1)}, bf16[1,128,1,4,64]{1,4,3,2,0:T(8,128)(2,1)S(1)}, u32[]{:S(2)}, u32[]{:S(2)}) collective-permute-start(bf16[1,128,1,4,64]{1,4,3,2,0:T(8,128)(2,1)S(1)} %get-tuple-element.29), channel_id=1, source_target_pairs={{1,0},{3,2},{5,4},{7,6},{9,8},{11,10},{13,12},{15,14},{17,16},{19,... | collective-permute-start | bytes 196616 | tf_op jit(solution)/shard_map/ppermute | solution.py:15
  87.0 0.6 fusion.196
  87.6 1.2 collective-permute-done.5
  93.8 0.9 broadcast_in_dim.16
  94.7 1.6 copy.88
  96.3 1.9 %multiply_convert_fusion = bf16[64,4,8,128]{3,0,2,1:T(8,128)(2,1)S(1)} fusion(f32[64,4,8,128]{3,0,2,1:T(8,128)} %copy.88, f32[64,4,8,128]{3,0,2,1:T(8,128)} %get-tuple-element.33), kind=kLoop, calls=%fused_computation.291 | loop fusion | flops 2359296 | bytes 2621440 | tf_op jit(solution)/shard_map/convert_element_type | solution.py:140
  106.5 30.5 %fusion.211 = (bf16[64,64]{1,0:T(8,128)(2,1)S(1)}, bf16[112,128]{1,0:T(8,128)(2,1)S(1)}) fusion(bf16[864,64]{1,0:T(8,128)(2,1)S(1)} %bitcast.1522, bf16[1728,128]{1,0:T(8,128)(2,1)S(1)} %bitcast.1521), kind=kCustom, calls=%all-reduce-scatter.2 | all-reduce-scatter fusion | flops 294914 | bytes 590336
  137.0 1.9 %collective-permute-start.8 = (bf16[64,64]{1,0:T(8,128)(2,1)S(1)}, bf16[64,64]{1,0:T(8,128)(2,1)S(1)}, u32[]{:S(2)}, u32[]{:S(2)}) collective-permute-start(bf16[64,64]{1,0:T(8,128)(2,1)S(1)} %get-tuple-element.20), channel_id=1, source_target_pairs={{0,2},{2,4},{4,6},{6,8},{8,10},{10,12},{12,14},{14,16},{16,18},{18... | collective-permute-start | bytes 24584
  138.9 1.9 %collective-permute-start.9 = (bf16[64,64]{1,0:T(8,128)(2,1)S(1)}, bf16[64,64]{1,0:T(8,128)(2,1)S(1)}, u32[]{:S(2)}, u32[]{:S(2)}) collective-permute-start(bf16[64,64]{1,0:T(8,128)(2,1)S(1)} %get-tuple-element.20), channel_id=1, source_target_pairs={{0,4},{2,6},{4,8},{6,10},{8,12},{10,14},{12,16},{14,18},{16,20},{1... | collective-permute-start | bytes 24584
  141.1 4.0 %collective-permute-start.11 = (bf16[60,128]{1,0:T(8,128)(2,1)S(1)}, bf16[60,128]{1,0:T(8,128)(2,1)S(1)}, u32[]{:S(2)}, u32[]{:S(2)}) collective-permute-start(bf16[60,128]{1,0:T(8,128)(2,1)S(1)} %slice.955), channel_id=1, source_target_pairs={{0,2},{2,4},{4,6},{6,8},{8,10},{10,12},{12,14},{14,16},{16,18},{18... | collective-permute-start | bytes 46088
  145.1 9.2 %collective-permute-start.10 = (bf16[22,64]{1,0:T(8,128)(2,1)S(1)}, bf16[22,64]{1,0:T(8,128)(2,1)S(1)}, u32[]{:S(2)}, u32[]{:S(2)}) collective-permute-start(bf16[22,64]{1,0:T(8,128)(2,1)S(1)} %slice.954), channel_id=1, source_target_pairs={{0,6},{2,8},{4,10},{6,12},{8,14},{10,16},{12,18},{14,20},{16,22},{... | collective-permute-start | bytes 8456
  154.3 3.9 %collective-permute-start.7 = (bf16[1,64,1,8,128]{4,1,3,2,0:T(8,128)(2,1)S(1)}, bf16[1,64,1,8,128]{4,1,3,2,0:T(8,128)(2,1)S(1)}, u32[]{:S(2)}, u32[]{:S(2)}) collective-permute-start(bf16[1,64,1,8,128]{4,1,3,2,0:T(8,128)(2,1)S(1)} %get-tuple-element.23), channel_id=1, source_target_pairs={{1,0},{3,2},{5,4},{7,6},{9,8},{11,10},{13,12},{15,14},{17,16},{19,... | collective-permute-start | bytes 393224 | tf_op jit(solution)/shard_map/ppermute | solution.py:15
  158.3 1.3 collective-permute-start.6
  159.6 0.6 concatenate.48
  160.5 9.7 %all-reduce.8 = (bf16[54,64]{1,0:T(8,128)(2,1)S(1)}, bf16[108,128]{1,0:T(8,128)(2,1)S(1)}) all-reduce(bf16[54,64]{1,0:T(8,128)(2,1)S(1)} %constant_dynamic-slice_fusion.1, bf16[108,128]{1,0:T(8,128)(2,1)S(1)} %constant_dynamic-slice_fusion), channel_id=1, replica_groups=mesh['dp'=16,'space'=2] {'space'}, use_global_device_ids=true, to_apply=%region_4.5 | all-reduce | flops 17280 | bytes 69120 | tf_op jit(solution)/shard_map/psum | solution.py:155
  170.3 0.6 convert_element_type.112
  170.9 0.6 convert_element_type.109
  171.5 1.1 select_maximum_fusion
  179.4 0.7 fusion.50
  180.5 0.5 fusion.76
  180.9 0.8 copy.117
  (191 shorter events, 36.8 us)
Async XLA Ops:
  1.7 23.5 %collective-permute-start = (bf16[1,32,1,8,128]{4,1,3,2,0:T(8,128)(2,1)S(1)}, bf16[1,32,1,8,128]{4,1,3,2,0:T(8,128)(2,1)S(1)}, u32[]{:S(2)}, u32[]{:S(2)}) collective-permute-start(bf16[1,32,1,8,128]{4,1,3,2,0:T(8,128)(2,1)S(1)} %get-tuple-element.26), channel_id=1, source_target_pairs={{0,1},{2,3},{4,5},{6,7},{8,9},{10,11},{12,13},{14,15},{16,17},{18,... | collective-permute-start | bytes 196616 | tf_op jit(solution)/shard_map/ppermute | solution.py:12
  3.0 22.2 %collective-permute-start.1 = (bf16[1,32,1,8,128]{4,1,3,2,0:T(8,128)(2,1)S(1)}, bf16[1,32,1,8,128]{4,1,3,2,0:T(8,128)(2,1)S(1)}, u32[]{:S(2)}, u32[]{:S(2)}) collective-permute-start(bf16[1,32,1,8,128]{4,1,3,2,0:T(8,128)(2,1)S(1)} %get-tuple-element.27), channel_id=1, source_target_pairs={{1,0},{3,2},{5,4},{7,6},{9,8},{11,10},{13,12},{15,14},{17,16},{19,... | collective-permute-start | bytes 196616 | tf_op jit(solution)/shard_map/ppermute | solution.py:15
  25.2 10.5 %copy-start.3 = (bf16[3,3,3,32,64]{4,3,2,1,0:T(8,128)(2,1)}, bf16[3,3,3,32,64]{4,3,2,1,0:T(8,128)(2,1)S(1)}, u32[]{:S(2)}) copy-start(bf16[3,3,3,32,64]{4,3,2,1,0:T(8,128)(2,1)S(1)} %reshape.915) | copy-start | bytes 331780
  33.4 1.0 copy-start.1
  39.4 9.3 %copy-start.6 = (bf16[108,128]{1,0:T(8,128)(2,1)S(1)}, bf16[108,128]{1,0:T(8,128)(2,1)}, u32[]{:S(2)}) copy-start(bf16[108,128]{1,0:T(8,128)(2,1)} %param.6) | copy-start | bytes 82948
  39.4 28.1 %copy-start.7 = (u32[32]{0:T(128)S(1)}, u32[32]{0:T(128)}, u32[]{:S(2)}) copy-start(u32[32]{0:T(128)} %constant.37) | copy-start | bytes 388
  42.9 26.6 %collective-permute-start.2 = (bf16[1,64,1,4,64]{1,4,3,2,0:T(8,128)(2,1)S(1)}, bf16[1,64,1,4,64]{1,4,3,2,0:T(8,128)(2,1)S(1)}, u32[]{:S(2)}, u32[]{:S(2)}) collective-permute-start(bf16[1,64,1,4,64]{1,4,3,2,0:T(8,128)(2,1)S(1)} %get-tuple-element.30), channel_id=1, source_target_pairs={{0,1},{2,3},{4,5},{6,7},{8,9},{10,11},{12,13},{14,15},{16,17},{18,... | collective-permute-start | bytes 98312 | tf_op jit(solution)/shard_map/ppermute | solution.py:12
  44.2 25.3 %collective-permute-start.3 = (bf16[1,64,1,4,64]{1,4,3,2,0:T(8,128)(2,1)S(1)}, bf16[1,64,1,4,64]{1,4,3,2,0:T(8,128)(2,1)S(1)}, u32[]{:S(2)}, u32[]{:S(2)}) collective-permute-start(bf16[1,64,1,4,64]{1,4,3,2,0:T(8,128)(2,1)S(1)} %get-tuple-element.31), channel_id=1, source_target_pairs={{1,0},{3,2},{5,4},{7,6},{9,8},{11,10},{13,12},{15,14},{17,16},{19,... | collective-permute-start | bytes 98312 | tf_op jit(solution)/shard_map/ppermute | solution.py:15
  71.3 1.0 copy-start
  81.1 6.6 %collective-permute-start.4 = (bf16[1,128,1,4,64]{1,4,3,2,0:T(8,128)(2,1)S(1)}, bf16[1,128,1,4,64]{1,4,3,2,0:T(8,128)(2,1)S(1)}, u32[]{:S(2)}, u32[]{:S(2)}) collective-permute-start(bf16[1,128,1,4,64]{1,4,3,2,0:T(8,128)(2,1)S(1)} %get-tuple-element.28), channel_id=1, source_target_pairs={{0,1},{2,3},{4,5},{6,7},{8,9},{10,11},{12,13},{14,15},{16,17},{18,... | collective-permute-start | bytes 196616 | tf_op jit(solution)/shard_map/ppermute | solution.py:12
  82.4 6.4 %collective-permute-start.5 = (bf16[1,128,1,4,64]{1,4,3,2,0:T(8,128)(2,1)S(1)}, bf16[1,128,1,4,64]{1,4,3,2,0:T(8,128)(2,1)S(1)}, u32[]{:S(2)}, u32[]{:S(2)}) collective-permute-start(bf16[1,128,1,4,64]{1,4,3,2,0:T(8,128)(2,1)S(1)} %get-tuple-element.29), channel_id=1, source_target_pairs={{1,0},{3,2},{5,4},{7,6},{9,8},{11,10},{13,12},{15,14},{17,16},{19,... | collective-permute-start | bytes 196616 | tf_op jit(solution)/shard_map/ppermute | solution.py:15
  100.6 1.5 copy-start.2
  105.2 1.3 copy-start.5
  105.5 35.4 %copy-start.4 = (bf16[3,3,3,32,64]{4,3,2,1,0:T(8,128)(2,1)S(1)}, bf16[3,3,3,32,64]{4,3,2,1,0:T(8,128)(2,1)}, u32[]{:S(2)}) copy-start(bf16[3,3,3,32,64]{4,3,2,1,0:T(8,128)(2,1)} %copy-done.3) | copy-start | bytes 331780
  137.0 22.6 %collective-permute-start.8 = (bf16[64,64]{1,0:T(8,128)(2,1)S(1)}, bf16[64,64]{1,0:T(8,128)(2,1)S(1)}, u32[]{:S(2)}, u32[]{:S(2)}) collective-permute-start(bf16[64,64]{1,0:T(8,128)(2,1)S(1)} %get-tuple-element.20), channel_id=1, source_target_pairs={{0,2},{2,4},{4,6},{6,8},{8,10},{10,12},{12,14},{14,16},{16,18},{18... | collective-permute-start | bytes 24584
  138.9 20.6 %collective-permute-start.9 = (bf16[64,64]{1,0:T(8,128)(2,1)S(1)}, bf16[64,64]{1,0:T(8,128)(2,1)S(1)}, u32[]{:S(2)}, u32[]{:S(2)}) collective-permute-start(bf16[64,64]{1,0:T(8,128)(2,1)S(1)} %get-tuple-element.20), channel_id=1, source_target_pairs={{0,4},{2,6},{4,8},{6,10},{8,12},{10,14},{12,16},{14,18},{16,20},{1... | collective-permute-start | bytes 24584
  141.1 19.1 %collective-permute-start.11 = (bf16[60,128]{1,0:T(8,128)(2,1)S(1)}, bf16[60,128]{1,0:T(8,128)(2,1)S(1)}, u32[]{:S(2)}, u32[]{:S(2)}) collective-permute-start(bf16[60,128]{1,0:T(8,128)(2,1)S(1)} %slice.955), channel_id=1, source_target_pairs={{0,2},{2,4},{4,6},{6,8},{8,10},{10,12},{12,14},{14,16},{16,18},{18... | collective-permute-start | bytes 46088
  145.1 13.1 %collective-permute-start.10 = (bf16[22,64]{1,0:T(8,128)(2,1)S(1)}, bf16[22,64]{1,0:T(8,128)(2,1)S(1)}, u32[]{:S(2)}, u32[]{:S(2)}) collective-permute-start(bf16[22,64]{1,0:T(8,128)(2,1)S(1)} %slice.954), channel_id=1, source_target_pairs={{0,6},{2,8},{4,10},{6,12},{8,14},{10,16},{12,18},{14,20},{16,22},{... | collective-permute-start | bytes 8456
  154.3 17.2 %collective-permute-start.7 = (bf16[1,64,1,8,128]{4,1,3,2,0:T(8,128)(2,1)S(1)}, bf16[1,64,1,8,128]{4,1,3,2,0:T(8,128)(2,1)S(1)}, u32[]{:S(2)}, u32[]{:S(2)}) collective-permute-start(bf16[1,64,1,8,128]{4,1,3,2,0:T(8,128)(2,1)S(1)} %get-tuple-element.23), channel_id=1, source_target_pairs={{1,0},{3,2},{5,4},{7,6},{9,8},{11,10},{13,12},{15,14},{17,16},{19,... | collective-permute-start | bytes 393224 | tf_op jit(solution)/shard_map/ppermute | solution.py:15
  158.3 13.2 %collective-permute-start.6 = (bf16[1,64,1,8,128]{4,1,3,2,0:T(8,128)(2,1)S(1)}, bf16[1,64,1,8,128]{4,1,3,2,0:T(8,128)(2,1)S(1)}, u32[]{:S(2)}, u32[]{:S(2)}) collective-permute-start(bf16[1,64,1,8,128]{4,1,3,2,0:T(8,128)(2,1)S(1)} %get-tuple-element.22), channel_id=1, source_target_pairs={{0,1},{2,3},{4,5},{6,7},{8,9},{10,11},{12,13},{14,15},{16,17},{18,... | collective-permute-start | bytes 393224 | tf_op jit(solution)/shard_map/ppermute | solution.py:12
where the time goes:
time: 182 us
  blocking collectives  75.8 us (42%)
  matrix products  43 us (24%)
  starting transfers between devices  39.7 us (22%)
  other arithmetic  10.6 us (6%)
  local copies, waits for them, and re-layouts  8.21 us (5%)
  between operations  3.1 us (2%)
    unnamed x1, blocking collectives  30.5 us
    all_gather x1, blocking collectives, local(): lax.all_gather(w_second, 'dp', axis=0, tiled=True)  18.7 us
    ppermute x4, starting transfers between devices, with_halo(): lax.ppermute(lax.slice_in_dim(block, 0, width, axis=dim), axis, backward)  17.6 us
    unnamed x4, starting transfers between devices  17 us
    all_gather x1, blocking collectives, local(): lax.all_gather(w_first, 'dp', axis=0, tiled=True)  16.8 us
    dot_general x54, matrix products, conv_forward(): jnp.einsum('sixyz,io->soxyz', window, kernel[along_x, along_y, along_z],...  16.1 us
    dot_general x54, matrix products, conv_weight_grad(): jnp.einsum('sixyz,soxyz->io', window, grads, preferred_element_type=jnp.f...  13.8 us
    dot_general x54, matrix products, conv_input_grad(): jnp.einsum('soxyz,io->sixyz', window, kernel[along_x, along_y, along_z],...  13.1 us
  transfers between devices with their start and end apart: 12, of which 1 were waited for; matrix products, arithmetic and copies ran while one was open for 2% of the time, Pallas kernels for 0%

commit v1 on v0

--- a/solution.py
+++ b/solution.py
@@ -2,6 +2,7 @@
 import jax.numpy as jnp
 from jax import lax
 from jax.sharding import PartitionSpec as P
+from jax.lax import all_gather
 
 
 def with_halo(block, sides, width):
@@ -152,7 +153,9 @@
         ).astype(jnp.float32),
     )
     share_one, share_two = (
-        lax.psum(rows_one.astype(jnp.bfloat16), "space").astype(jnp.float32),
+        jnp.sum(all_gather(rows_one.astype(jnp.bfloat16), axis_name="space"), axis=0).astype(
+            jnp.float32
+        ),
         lax.psum(rows_two.astype(jnp.bfloat16), "space").astype(jnp.float32),
     )
     return (pooled, volume_grad, share_one, share_two)

time: 182 us -> 187 us (1.027)
  blocking collectives: 75.8 us -> 80 us
    all_gather x0 -> x1, blocking collectives: none -> 5.12 us  [local(): all_gather(rows_one.astype(jnp.bfloat16), axis_name='space')]
where the time goes in v1:
time: 187 us; the launch traced here: 186 us
  blocking collectives  80 us (43%)
  matrix products  43 us (23%)
  starting transfers between devices  39.7 us (21%)
  other arithmetic  10.6 us (6%)
  local copies, waits for them, and re-layouts  8.23 us (4%)
  between operations  3.09 us (2%)
    unnamed x1, blocking collectives  30.5 us
    all_gather x1, blocking collectives, local(): lax.all_gather(w_second, 'dp', axis=0, tiled=True)  18.7 us
    ppermute x4, starting transfers between devices, with_halo(): lax.ppermute(lax.slice_in_dim(block, 0, width, axis=dim), axis, backward)  17.6 us
    unnamed x4, starting transfers between devices  17 us
    all_gather x1, blocking collectives, local(): lax.all_gather(w_first, 'dp', axis=0, tiled=True)  16.8 us
    dot_general x54, matrix products, conv_forward(): jnp.einsum('sixyz,io->soxyz', window, kernel[along_x, along_y, along_z],...  16.1 us
    dot_general x54, matrix products, conv_weight_grad(): jnp.einsum('sixyz,soxyz->io', window, grads, preferred_element_type=jnp.f...  13.8 us
    dot_general x54, matrix products, conv_input_grad(): jnp.einsum('soxyz,io->sixyz', window, kernel[along_x, along_y, along_z],...  13.1 us
  transfers between devices with their start and end apart: 12, of which 1 were waited for; matrix products, arithmetic and copies ran while one was open for 2% of the time, Pallas kernels for 0%

profile of v1, /device:TPU:18, one launch (start us, length us, event | category | flops | bytes accessed | tf_op | source)
XLA Modules:
  0.0 185.9 jit_solution(1503995329860898905)
XLA Ops:
  0.6 1.1 copy.81
  1.7 1.3 collective-permute-start
  3.0 4.5 %collective-permute-start.1 = (bf16[1,32,1,8,128]{4,1,3,2,0:T(8,128)(2,1)S(1)}, bf16[1,32,1,8,128]{4,1,3,2,0:T(8,128)(2,1)S(1)}, u32[]{:S(2)}, u32[]{:S(2)}) collective-permute-start(bf16[1,32,1,8,128]{4,1,3,2,0:T(8,128)(2,1)S(1)} %get-tuple-element.25), channel_id=1, source_target_pairs={{1,0},{3,2},{5,4},{7,6},{9,8},{11,10},{13,12},{15,14},{17,16},{19,... | collective-permute-start | bytes 196616 | tf_op jit(solution)/shard_map/ppermute | solution.py:16
  7.6 0.7 multiply_bitcast_fusion
  8.3 16.8 %all-gather.1 = bf16[16,54,64]{2,1,0:T(8,128)(2,1)S(1)} all-gather(bf16[1,54,64]{2,1,0:T(8,128)(2,1)} %bitcast.1528), channel_id=1, replica_groups=mesh['dp'=16,'space'=2] {'dp'}, dimensions={0}, use_global_device_ids=true | all-gather | bytes 117504 | tf_op jit(solution)/shard_map/all_gather | solution.py:121
  25.2 0.4 select_maximum_fusion.2
  26.0 0.4 fusion.173
  26.4 0.4 convolution_bitcast_fusion.10
  27.1 0.4 convolution_bitcast_fusion.6
  28.2 0.4 convolution_bitcast_fusion.9
  29.0 0.4 convolution_bitcast_fusion.1
  30.5 0.4 convolution_add_fusion.10
  31.9 0.4 convolution_add_fusion.6
  33.0 0.4 convolution_add_fusion.3
  33.4 0.4 convolution_add_fusion.2
  34.7 0.6 fusion.17
  35.7 2.0 %fusion.134 = (f32[64,4,8,128]{3,0,2,1:T(8,128)}, f32[64,4,8,128]{3,0,2,1:T(8,128)}) fusion(f32[64,4,8,128]{3,0,2,1:T(8,128)S(1)} %convolution_bitcast_fusion, f32[64,4,8,128]{3,0,2,1:T(8,128)S(1)} %convolution_bitcast_fusion.1, f32[64,4,8,128]{3,0,2,1:T(8,128)S(1)} %convolution_bitcast_fusion.2, f32[64,4,8,128]{3,0,2,1:T(8,128)S(1)} %convolution_bitcast_fusion.3, ...), kind=kOutput, calls=%fused_computation.293 | convolution fusion | flops 19267584 | bytes 7675904 | tf_op jit(solution)/shard_map/sixyz,io->soxyz/dot_general | solution.py:42
  37.6 1.8 copy.87
  39.5 2.4 %reduce_sum.37 = f32[64,2,4,64]{0,3,2,1:T(8,128)} reduce(f32[64,2,2,4,2,64,2]{0,6,5,4,3,2,1:T(2,128)S(1)} %bitcast.1519, f32[]{:T(128)} %constant.8.clone.1), dimensions={2,4,6}, to_apply=%region_0.1 | reduce | flops 229376 | bytes 1179652 | tf_op jit(solution)/shard_map/reduce_sum | solution.py:102
  41.9 1.0 fusion.210
  42.9 1.3 collective-permute-start.2
  44.2 4.5 %collective-permute-start.3 = (bf16[1,64,1,4,64]{1,4,3,2,0:T(8,128)(2,1)S(1)}, bf16[1,64,1,4,64]{1,4,3,2,0:T(8,128)(2,1)S(1)}, u32[]{:S(2)}, u32[]{:S(2)}) collective-permute-start(bf16[1,64,1,4,64]{1,4,3,2,0:T(8,128)(2,1)S(1)} %get-tuple-element.29), channel_id=1, source_target_pairs={{1,0},{3,2},{5,4},{7,6},{9,8},{11,10},{13,12},{15,14},{17,16},{19,... | collective-permute-start | bytes 98312 | tf_op jit(solution)/shard_map/ppermute | solution.py:16
  48.8 18.7 %all-gather.2 = bf16[16,108,128]{2,1,0:T(8,128)(2,1)S(1)} all-gather(bf16[1,108,128]{2,1,0:T(8,128)(2,1)S(1)} %bitcast.1527), channel_id=1, replica_groups=mesh['dp'=16,'space'=2] {'dp'}, dimensions={0}, use_global_device_ids=true | all-gather | bytes 470016 | tf_op jit(solution)/shard_map/all_gather | solution.py:122
  67.6 0.6 dynamic-slice.6
  80.2 0.9 multiply_convert_fusion.1
  81.1 1.3 collective-permute-start.4
  82.4 4.5 %collective-permute-start.5 = (bf16[1,128,1,4,64]{1,4,3,2,0:T(8,128)(2,1)S(1)}, bf16[1,128,1,4,64]{1,4,3,2,0:T(8,128)(2,1)S(1)}, u32[]{:S(2)}, u32[]{:S(2)}) collective-permute-start(bf16[1,128,1,4,64]{1,4,3,2,0:T(8,128)(2,1)S(1)} %get-tuple-element.27), channel_id=1, source_target_pairs={{1,0},{3,2},{5,4},{7,6},{9,8},{11,10},{13,12},{15,14},{17,16},{19,... | collective-permute-start | bytes 196616 | tf_op jit(solution)/shard_map/ppermute | solution.py:16
  87.0 0.6 fusion.196
  87.6 1.2 collective-permute-done.5
  93.8 0.9 broadcast_in_dim.16
  94.7 1.6 copy.88
  96.3 1.9 %multiply_convert_fusion = bf16[64,4,8,128]{3,0,2,1:T(8,128)(2,1)S(1)} fusion(f32[64,4,8,128]{3,0,2,1:T(8,128)} %copy.88, f32[64,4,8,128]{3,0,2,1:T(8,128)} %get-tuple-element.31), kind=kLoop, calls=%fused_computation.291 | loop fusion | flops 2359296 | bytes 2621440 | tf_op jit(solution)/shard_map/convert_element_type | solution.py:141
  106.5 30.5 %fusion.211 = (bf16[64,64]{1,0:T(8,128)(2,1)S(1)}, bf16[112,128]{1,0:T(8,128)(2,1)S(1)}) fusion(bf16[864,64]{1,0:T(8,128)(2,1)S(1)} %bitcast.1524, bf16[1728,128]{1,0:T(8,128)(2,1)S(1)} %bitcast.1523), kind=kCustom, calls=%all-reduce-scatter.2 | all-reduce-scatter fusion | flops 294914 | bytes 590336
  137.0 1.9 %collective-permute-start.8 = (bf16[64,64]{1,0:T(8,128)(2,1)S(1)}, bf16[64,64]{1,0:T(8,128)(2,1)S(1)}, u32[]{:S(2)}, u32[]{:S(2)}) collective-permute-start(bf16[64,64]{1,0:T(8,128)(2,1)S(1)} %get-tuple-element.18), channel_id=1, source_target_pairs={{0,2},{2,4},{4,6},{6,8},{8,10},{10,12},{12,14},{14,16},{16,18},{18... | collective-permute-start | bytes 24584
  139.0 1.9 %collective-permute-start.9 = (bf16[64,64]{1,0:T(8,128)(2,1)S(1)}, bf16[64,64]{1,0:T(8,128)(2,1)S(1)}, u32[]{:S(2)}, u32[]{:S(2)}) collective-permute-start(bf16[64,64]{1,0:T(8,128)(2,1)S(1)} %get-tuple-element.18), channel_id=1, source_target_pairs={{0,4},{2,6},{4,8},{6,10},{8,12},{10,14},{12,16},{14,18},{16,20},{1... | collective-permute-start | bytes 24584
  141.1 4.0 %collective-permute-start.11 = (bf16[60,128]{1,0:T(8,128)(2,1)S(1)}, bf16[60,128]{1,0:T(8,128)(2,1)S(1)}, u32[]{:S(2)}, u32[]{:S(2)}) collective-permute-start(bf16[60,128]{1,0:T(8,128)(2,1)S(1)} %slice.955), channel_id=1, source_target_pairs={{0,2},{2,4},{4,6},{6,8},{8,10},{10,12},{12,14},{14,16},{16,18},{18... | collective-permute-start | bytes 46088
  145.1 9.2 %collective-permute-start.10 = (bf16[22,64]{1,0:T(8,128)(2,1)S(1)}, bf16[22,64]{1,0:T(8,128)(2,1)S(1)}, u32[]{:S(2)}, u32[]{:S(2)}) collective-permute-start(bf16[22,64]{1,0:T(8,128)(2,1)S(1)} %slice.954), channel_id=1, source_target_pairs={{0,6},{2,8},{4,10},{6,12},{8,14},{10,16},{12,18},{14,20},{16,22},{... | collective-permute-start | bytes 8456
  154.4 3.9 %collective-permute-start.7 = (bf16[1,64,1,8,128]{4,1,3,2,0:T(8,128)(2,1)S(1)}, bf16[1,64,1,8,128]{4,1,3,2,0:T(8,128)(2,1)S(1)}, u32[]{:S(2)}, u32[]{:S(2)}) collective-permute-start(bf16[1,64,1,8,128]{4,1,3,2,0:T(8,128)(2,1)S(1)} %get-tuple-element.21), channel_id=1, source_target_pairs={{1,0},{3,2},{5,4},{7,6},{9,8},{11,10},{13,12},{15,14},{17,16},{19,... | collective-permute-start | bytes 393224 | tf_op jit(solution)/shard_map/ppermute | solution.py:16
  158.3 1.3 collective-permute-start.6
  159.6 0.6 concatenate.48
  160.2 5.1 %all-gather.3 = bf16[2,54,64]{2,1,0:T(8,128)(2,1)S(1)} all-gather(bf16[1,54,64]{2,1,0:T(8,128)(2,1)S(1)} %dynamic-slice_bitcast_fusion), channel_id=2, replica_groups=mesh['dp'=16,'space'=2] {'space'}, dimensions={0}, use_global_device_ids=true | all-gather | bytes 20736 | tf_op jit(solution)/shard_map/all_gather | solution.py:156
  165.4 0.6 convert_element_type.111
  166.3 8.8 %psum.7 = bf16[108,128]{1,0:T(8,128)(2,1)S(1)} all-reduce(bf16[108,128]{1,0:T(8,128)(2,1)S(1)} %constant_dynamic-slice_fusion), channel_id=1, replica_groups=mesh['dp'=16,'space'=2] {'space'}, use_global_device_ids=true, to_apply=%region_6.7 | all-reduce | flops 13824 | bytes 55296 | tf_op jit(solution)/shard_map/psum | solution.py:159
  175.1 0.6 convert_element_type.114
  175.7 1.1 select_maximum_fusion
  183.5 0.7 fusion.50
  184.6 0.5 fusion.76
  185.1 0.8 copy.117
  (193 shorter events, 37.2 us)
Async XLA Ops:
  1.7 23.5 %collective-permute-start = (bf16[1,32,1,8,128]{4,1,3,2,0:T(8,128)(2,1)S(1)}, bf16[1,32,1,8,128]{4,1,3,2,0:T(8,128)(2,1)S(1)}, u32[]{:S(2)}, u32[]{:S(2)}) collective-permute-start(bf16[1,32,1,8,128]{4,1,3,2,0:T(8,128)(2,1)S(1)} %get-tuple-element.24), channel_id=1, source_target_pairs={{0,1},{2,3},{4,5},{6,7},{8,9},{10,11},{12,13},{14,15},{16,17},{18,... | collective-permute-start | bytes 196616 | tf_op jit(solution)/shard_map/ppermute | solution.py:13
  3.0 22.2 %collective-permute-start.1 = (bf16[1,32,1,8,128]{4,1,3,2,0:T(8,128)(2,1)S(1)}, bf16[1,32,1,8,128]{4,1,3,2,0:T(8,128)(2,1)S(1)}, u32[]{:S(2)}, u32[]{:S(2)}) collective-permute-start(bf16[1,32,1,8,128]{4,1,3,2,0:T(8,128)(2,1)S(1)} %get-tuple-element.25), channel_id=1, source_target_pairs={{1,0},{3,2},{5,4},{7,6},{9,8},{11,10},{13,12},{15,14},{17,16},{19,... | collective-permute-start | bytes 196616 | tf_op jit(solution)/shard_map/ppermute | solution.py:16
  25.2 10.5 %copy-start.3 = (bf16[3,3,3,32,64]{4,3,2,1,0:T(8,128)(2,1)}, bf16[3,3,3,32,64]{4,3,2,1,0:T(8,128)(2,1)S(1)}, u32[]{:S(2)}) copy-start(bf16[3,3,3,32,64]{4,3,2,1,0:T(8,128)(2,1)S(1)} %reshape.915) | copy-start | bytes 331780
  33.4 1.0 copy-start.1
  39.5 9.3 %copy-start.6 = (bf16[108,128]{1,0:T(8,128)(2,1)S(1)}, bf16[108,128]{1,0:T(8,128)(2,1)}, u32[]{:S(2)}) copy-start(bf16[108,128]{1,0:T(8,128)(2,1)} %param.6) | copy-start | bytes 82948
  39.5 28.1 %copy-start.7 = (u32[32]{0:T(128)S(1)}, u32[32]{0:T(128)}, u32[]{:S(2)}) copy-start(u32[32]{0:T(128)} %constant.38) | copy-start | bytes 388
  42.9 26.6 %collective-permute-start.2 = (bf16[1,64,1,4,64]{1,4,3,2,0:T(8,128)(2,1)S(1)}, bf16[1,64,1,4,64]{1,4,3,2,0:T(8,128)(2,1)S(1)}, u32[]{:S(2)}, u32[]{:S(2)}) collective-permute-start(bf16[1,64,1,4,64]{1,4,3,2,0:T(8,128)(2,1)S(1)} %get-tuple-element.28), channel_id=1, source_target_pairs={{0,1},{2,3},{4,5},{6,7},{8,9},{10,11},{12,13},{14,15},{16,17},{18,... | collective-permute-start | bytes 98312 | tf_op jit(solution)/shard_map/ppermute | solution.py:13
  44.2 25.3 %collective-permute-start.3 = (bf16[1,64,1,4,64]{1,4,3,2,0:T(8,128)(2,1)S(1)}, bf16[1,64,1,4,64]{1,4,3,2,0:T(8,128)(2,1)S(1)}, u32[]{:S(2)}, u32[]{:S(2)}) collective-permute-start(bf16[1,64,1,4,64]{1,4,3,2,0:T(8,128)(2,1)S(1)} %get-tuple-element.29), channel_id=1, source_target_pairs={{1,0},{3,2},{5,4},{7,6},{9,8},{11,10},{13,12},{15,14},{17,16},{19,... | collective-permute-start | bytes 98312 | tf_op jit(solution)/shard_map/ppermute | solution.py:16
  71.3 1.0 copy-start
  81.1 6.6 %collective-permute-start.4 = (bf16[1,128,1,4,64]{1,4,3,2,0:T(8,128)(2,1)S(1)}, bf16[1,128,1,4,64]{1,4,3,2,0:T(8,128)(2,1)S(1)}, u32[]{:S(2)}, u32[]{:S(2)}) collective-permute-start(bf16[1,128,1,4,64]{1,4,3,2,0:T(8,128)(2,1)S(1)} %get-tuple-element.26), channel_id=1, source_target_pairs={{0,1},{2,3},{4,5},{6,7},{8,9},{10,11},{12,13},{14,15},{16,17},{18,... | collective-permute-start | bytes 196616 | tf_op jit(solution)/shard_map/ppermute | solution.py:13
  82.4 6.4 %collective-permute-start.5 = (bf16[1,128,1,4,64]{1,4,3,2,0:T(8,128)(2,1)S(1)}, bf16[1,128,1,4,64]{1,4,3,2,0:T(8,128)(2,1)S(1)}, u32[]{:S(2)}, u32[]{:S(2)}) collective-permute-start(bf16[1,128,1,4,64]{1,4,3,2,0:T(8,128)(2,1)S(1)} %get-tuple-element.27), channel_id=1, source_target_pairs={{1,0},{3,2},{5,4},{7,6},{9,8},{11,10},{13,12},{15,14},{17,16},{19,... | collective-permute-start | bytes 196616 | tf_op jit(solution)/shard_map/ppermute | solution.py:16
  100.6 1.5 copy-start.2
  105.2 1.3 copy-start.5
  105.5 35.4 %copy-start.4 = (bf16[3,3,3,32,64]{4,3,2,1,0:T(8,128)(2,1)S(1)}, bf16[3,3,3,32,64]{4,3,2,1,0:T(8,128)(2,1)}, u32[]{:S(2)}) copy-start(bf16[3,3,3,32,64]{4,3,2,1,0:T(8,128)(2,1)} %copy-done.3) | copy-start | bytes 331780
  137.0 22.6 %collective-permute-start.8 = (bf16[64,64]{1,0:T(8,128)(2,1)S(1)}, bf16[64,64]{1,0:T(8,128)(2,1)S(1)}, u32[]{:S(2)}, u32[]{:S(2)}) collective-permute-start(bf16[64,64]{1,0:T(8,128)(2,1)S(1)} %get-tuple-element.18), channel_id=1, source_target_pairs={{0,2},{2,4},{4,6},{6,8},{8,10},{10,12},{12,14},{14,16},{16,18},{18... | collective-permute-start | bytes 24584
  139.0 20.6 %collective-permute-start.9 = (bf16[64,64]{1,0:T(8,128)(2,1)S(1)}, bf16[64,64]{1,0:T(8,128)(2,1)S(1)}, u32[]{:S(2)}, u32[]{:S(2)}) collective-permute-start(bf16[64,64]{1,0:T(8,128)(2,1)S(1)} %get-tuple-element.18), channel_id=1, source_target_pairs={{0,4},{2,6},{4,8},{6,10},{8,12},{10,14},{12,16},{14,18},{16,20},{1... | collective-permute-start | bytes 24584
  141.1 24.8 %collective-permute-start.11 = (bf16[60,128]{1,0:T(8,128)(2,1)S(1)}, bf16[60,128]{1,0:T(8,128)(2,1)S(1)}, u32[]{:S(2)}, u32[]{:S(2)}) collective-permute-start(bf16[60,128]{1,0:T(8,128)(2,1)S(1)} %slice.955), channel_id=1, source_target_pairs={{0,2},{2,4},{4,6},{6,8},{8,10},{10,12},{12,14},{14,16},{16,18},{18... | collective-permute-start | bytes 46088
  145.1 13.1 %collective-permute-start.10 = (bf16[22,64]{1,0:T(8,128)(2,1)S(1)}, bf16[22,64]{1,0:T(8,128)(2,1)S(1)}, u32[]{:S(2)}, u32[]{:S(2)}) collective-permute-start(bf16[22,64]{1,0:T(8,128)(2,1)S(1)} %slice.954), channel_id=1, source_target_pairs={{0,6},{2,8},{4,10},{6,12},{8,14},{10,16},{12,18},{14,20},{16,22},{... | collective-permute-start | bytes 8456
  154.4 21.3 %collective-permute-start.7 = (bf16[1,64,1,8,128]{4,1,3,2,0:T(8,128)(2,1)S(1)}, bf16[1,64,1,8,128]{4,1,3,2,0:T(8,128)(2,1)S(1)}, u32[]{:S(2)}, u32[]{:S(2)}) collective-permute-start(bf16[1,64,1,8,128]{4,1,3,2,0:T(8,128)(2,1)S(1)} %get-tuple-element.21), channel_id=1, source_target_pairs={{1,0},{3,2},{5,4},{7,6},{9,8},{11,10},{13,12},{15,14},{17,16},{19,... | collective-permute-start | bytes 393224 | tf_op jit(solution)/shard_map/ppermute | solution.py:16
  158.3 17.4 %collective-permute-start.6 = (bf16[1,64,1,8,128]{4,1,3,2,0:T(8,128)(2,1)S(1)}, bf16[1,64,1,8,128]{4,1,3,2,0:T(8,128)(2,1)S(1)}, u32[]{:S(2)}, u32[]{:S(2)}) collective-permute-start(bf16[1,64,1,8,128]{4,1,3,2,0:T(8,128)(2,1)S(1)} %get-tuple-element.20), channel_id=1, source_target_pairs={{0,1},{2,3},{4,5},{6,7},{8,9},{10,11},{12,13},{14,15},{16,17},{18,... | collective-permute-start | bytes 393224 | tf_op jit(solution)/shard_map/ppermute | solution.py:13
